TPU v7x, 32 devices: a whole 2x2x4 slice. The times are simulated.
32 devices in a mesh: groups: 2 (over x), tm: 16 (over z, y, core).
Axes of the slice: x: 2, y: 2, z: 4, core: 2. Of those that a mesh axis runs over, the one named last changes fastest.
Arguments:
- points: float32 [32, 64, 2048], P(('groups', 'tm')), parts along dimension 0, may hold values from -4 to 4
- potentials: float32 [32, 224, 2048], P(('groups', 'tm')), parts along dimension 0, may hold values from 0.5 to 25, as said below
- supports: int32 [32], P(('groups', 'tm')), parts along dimension 0, may hold values from 512 to 2048, as said below
Outputs:
- messages: float32 [32, 224, 2048], P(('groups', 'tm')), parts along dimension 0
- log_scale: float32 [448], P('groups'), parts along dimension 0
There are 2 independent parts, one for each index of `groups`. A program takes and returns all parts, laid end to end along the dimension named above; each array names one. Nothing has to cross between parts.
Inputs may be any that keep to these rules, and one draw needn't show every extreme that they name: `supports`: the first and the last time slice have all 2048 points live; every other slice has between 512 and 1024 live points, at its first positions. `potentials`: positive scalings.
All inputs are finite; a program needn't handle non-finite values.
Results may differ from a plain program's by a relative error of at most 0.017.
Values may be sent and summed in bfloat16 or wider, within the bound.
No kernel may reach another device: no remote copies, remote signals or barrier semaphores. Data moves between devices by JAX's collectives and lax.ppermute only.
A program may use at most 64 MiB of HBM per device.

v0:
```python
import jax
import jax.numpy as jnp
from jax import lax
from jax.sharding import PartitionSpec as P

MICRO = 32
A_DECAY = 0.8
EPS_SCALE = 0.05


def shifted(value, axis, steps):
    count = lax.axis_size(axis)
    initial, last = (max(0, -steps), min(count, count - steps))
    return lax.ppermute(value, axis, [(source, source + steps) for source in range(initial, last)])


def slice_kernel(source, target):
    dim_count, point_count = source.shape
    block_rows = min(512, point_count)
    inv_width = 1.0 / (2.0 * EPS_SCALE * dim_count)
    target_sq = jnp.sum(target * target, axis=0)
    pieces = jnp.transpose(
        source.reshape(dim_count, point_count // block_rows, block_rows), (1, 0, 2)
    )

    def one_block(segment):
        products = lax.dot_general(
            segment,
            target,
            (((0,), (0,)), ((), ())),
            precision=lax.Precision.HIGHEST,
            preferred_element_type=jnp.float32,
        )
        segment_sq = jnp.sum(segment * segment, axis=0)
        distance = (
            target_sq[None, :] + A_DECAY * A_DECAY * segment_sq[:, None] - 2.0 * A_DECAY * products
        )
        return jnp.exp(-inv_width * distance).astype(jnp.bfloat16)

    return lax.map(one_block, pieces).reshape(point_count, point_count)


def push_forward(weighted, kernel, live_row):
    pushed = jnp.dot(weighted, kernel, preferred_element_type=jnp.float32) * live_row[None, :]
    return (pushed, jnp.sum(pushed, axis=1))


def per_device(points, potentials, supports):
    local_slices, dim_count, point_count = points.shape
    all_cols = potentials.shape[1]
    tm_count = lax.axis_size("tm")
    position = lax.axis_index("tm")
    live_mask = (jnp.arange(point_count, dtype=jnp.int32)[None, :] < supports[:, None]).astype(
        jnp.float32
    )
    counts = supports.astype(jnp.float32)
    arrived = shifted(points[local_slices - 1], "tm", 1)
    sources = jnp.concatenate([arrived[None], points[:-1]], axis=0)
    kernels = lax.map(lambda paired: slice_kernel(paired[0], paired[1]), (sources, points))
    block_cols = MICRO
    batches = all_cols // block_cols
    phase_count = tm_count + batches - 1
    is_first = position == 0

    def section(incoming, block_id):
        block_pot = lax.dynamic_slice_in_dim(potentials, block_id * block_cols, block_cols, 1)
        pushed, column_sum = push_forward(incoming, kernels[0], live_mask[0])
        safe_sum = jnp.where(is_first, 1.0, column_sum)
        start_msg = jnp.broadcast_to(live_mask[0][None, :], pushed.shape)
        message = jnp.where(is_first, start_msg, pushed * (counts[0] / safe_sum)[:, None])
        outputs = [message]
        log_terms = [jnp.where(is_first, 0.0, jnp.log(safe_sum / counts[0]))]
        outgoing = (message * block_pot[local_slices - 1]).astype(jnp.bfloat16)
        return (jnp.stack(outputs), jnp.stack(log_terms), outgoing)

    def advance(phase, state_in):
        incoming, messages, log_parts = state_in
        block_id = phase - position
        active = (block_id >= 0) & (block_id < batches)
        clipped = jnp.clip(block_id, 0, batches - 1)

        def compute(operands):
            stored, stored_logs = operands
            block_msgs, block_logs, outgoing = section(incoming, clipped)
            stored = lax.dynamic_update_slice_in_dim(stored, block_msgs, clipped * block_cols, 1)
            stored_logs = lax.dynamic_update_slice_in_dim(
                stored_logs, block_logs, clipped * block_cols, 1
            )
            return (stored, stored_logs, outgoing)

        def skipped(operands):
            stored, stored_logs = operands
            return (stored, stored_logs, jnp.zeros((block_cols, point_count), jnp.bfloat16))

        messages, log_parts, outgoing = lax.cond(active, compute, skipped, (messages, log_parts))
        received = shifted(outgoing, "tm", 1)
        return (received, messages, log_parts)

    initial = (
        jnp.zeros((block_cols, point_count), jnp.bfloat16),
        jnp.zeros((local_slices, all_cols, point_count), jnp.float32),
        jnp.zeros((local_slices, all_cols), jnp.float32),
    )
    unused, messages, log_parts = lax.fori_loop(0, phase_count, advance, initial)
    local_log = jnp.sum(log_parts, axis=0)
    log_scale = lax.psum(local_log, "tm") / (tm_count * local_slices - 1)
    return (messages, log_scale)


def solution(mesh):
    placed = (P(("groups", "tm"), None, None), P(("groups", "tm"), None, None), P(("groups", "tm")))
    return jax.shard_map(
        per_device,
        mesh=mesh,
        in_specs=placed,
        out_specs=(P(("groups", "tm"), None, None), P("groups")),
        check_vma=False,
    )
```

profile of v0, /device:TPU:0, one launch (start us, length us, event | category | flops | bytes accessed | tf_op | source)
XLA Modules:
  0.0 334.8 jit_solution(13703646366627489090)
XLA Ops:
  4.9 26.2 %while.35 = (s32[]{:T(128)}, bf16[4,512,2048]{2,1,0:T(8,128)(2,1)}, f32[2048]{0:T(1024)S(1)}, f32[4,64,512]{2,1,0:T(8,128)S(1)}, f32[64,2048]{1,0:T(8,128)}, /*index=5*/s32[]{:T(128)}) while((s32[]{:T(128)}, bf16[4,512,2048]{2,1,0:T(8,128)(2,1)}, f32[2048]{0:T(1024)S(1)}, f32[4,64,512]{2,1,0:T(8,128)S(1)}, f32[64,2048]{1,0:T(8,128)}, ...), condition=%wide.region_3.0_spmd, body=%wide.region_1.3_spmd.sunk | while | flops 810614784 | bytes 2901065 | solution.py:40
  4.9 6.5 %fusion.26 = bf16[4,512,2048]{2,1,0:T(8,128)(2,1)} fusion(bf16[4,512,2048]{2,1,0:T(8,128)(2,1)} %get-tuple-element.449, s32[]{:T(128)} %get-tuple-element.448, f32[64,2048]{1,0:T(8,128)} %get-tuple-element.458, f32[512]{0:T(512)S(1)} %broadcast_multiply_fusion.3, f32[2048]{0:T(1024)S(1)} %get-tuple-element.456, f32[4,64,512]{2,1,0:T(8,128)S(1)} %get-tuple-element.457), kind=kOutput, calls=%fused_computation.3.clone.1 | convolution fusion | flops 810549248 | bytes 2763776 | tf_op jit(solution)/shard_map/while/body/eval_jaxpr/while/body/eval_jaxpr/dot_general | solution.py:27
  11.5 6.5 %fusion.26 = bf16[4,512,2048]{2,1,0:T(8,128)(2,1)} fusion(bf16[4,512,2048]{2,1,0:T(8,128)(2,1)} %get-tuple-element.449, s32[]{:T(128)} %get-tuple-element.448, f32[64,2048]{1,0:T(8,128)} %get-tuple-element.458, f32[512]{0:T(512)S(1)} %broadcast_multiply_fusion.3, f32[2048]{0:T(1024)S(1)} %get-tuple-element.456, f32[4,64,512]{2,1,0:T(8,128)S(1)} %get-tuple-element.457), kind=kOutput, calls=%fused_computation.3.clone.1 | convolution fusion | flops 810549248 | bytes 2763776 | tf_op jit(solution)/shard_map/while/body/eval_jaxpr/while/body/eval_jaxpr/dot_general | solution.py:27
  18.1 6.5 %fusion.26 = bf16[4,512,2048]{2,1,0:T(8,128)(2,1)} fusion(bf16[4,512,2048]{2,1,0:T(8,128)(2,1)} %get-tuple-element.449, s32[]{:T(128)} %get-tuple-element.448, f32[64,2048]{1,0:T(8,128)} %get-tuple-element.458, f32[512]{0:T(512)S(1)} %broadcast_multiply_fusion.3, f32[2048]{0:T(1024)S(1)} %get-tuple-element.456, f32[4,64,512]{2,1,0:T(8,128)S(1)} %get-tuple-element.457), kind=kOutput, calls=%fused_computation.3.clone.1 | convolution fusion | flops 810549248 | bytes 2763776 | tf_op jit(solution)/shard_map/while/body/eval_jaxpr/while/body/eval_jaxpr/dot_general | solution.py:27
  24.6 6.5 %fusion.26 = bf16[4,512,2048]{2,1,0:T(8,128)(2,1)} fusion(bf16[4,512,2048]{2,1,0:T(8,128)(2,1)} %get-tuple-element.449, s32[]{:T(128)} %get-tuple-element.448, f32[64,2048]{1,0:T(8,128)} %get-tuple-element.458, f32[512]{0:T(512)S(1)} %broadcast_multiply_fusion.3, f32[2048]{0:T(1024)S(1)} %get-tuple-element.456, f32[4,64,512]{2,1,0:T(8,128)S(1)} %get-tuple-element.457), kind=kOutput, calls=%fused_computation.3.clone.1 | convolution fusion | flops 810549248 | bytes 2763776 | tf_op jit(solution)/shard_map/while/body/eval_jaxpr/while/body/eval_jaxpr/dot_general | solution.py:27
  31.4 226.2 %while.36 = (s32[]{:T(128)}, bf16[32,2048]{1,0:T(8,128)(2,1)S(1)}, f32[1,224,2048]{2,1,0:T(8,128)S(1)}, f32[1,224]{1,0:T(1,128)S(1)}, s32[]{:T(128)}, /*index=5*...) while((s32[]{:T(128)}, bf16[32,2048]{1,0:T(8,128)(2,1)S(1)}, ...), condition=%wide.region_8.9_spmd.clone, body=%wide.region_4.8_spmd.clone.sunk | while | flops 268963936 | bytes 10520344 | solution.py:104
  32.0 6.4 %conditional.3 = (f32[1,224,2048]{2,1,0:T(8,128)S(1)}, f32[1,224]{1,0:T(1,128)S(1)}, bf16[32,2048]{1,0:T(8,128)(2,1)S(1)}) conditional(s32[]{:T(128)} %convert_element_type.47, (f32[1,224,2048]{2,1,0:T(8,128)S(1)}, f32[1,224]{1,0:T(1,128)S(1)}) %tuple.68, (pred[]{:T(512)}, f32[1,2048]{1,0:T(1,128)S(1)}, bf16[1,2048,2048]{2,1,0:T(8,128)(2,1)}, ...), branch_computations={%region_5.5_spmd, %region_6.7_spmd} | conditional | flops 268959840 | bytes 9987569 | solution.py:95
  42.9 6.5 %conditional.3 = (f32[1,224,2048]{2,1,0:T(8,128)S(1)}, f32[1,224]{1,0:T(1,128)S(1)}, bf16[32,2048]{1,0:T(8,128)(2,1)S(1)}) conditional(s32[]{:T(128)} %convert_element_type.47, (f32[1,224,2048]{2,1,0:T(8,128)S(1)}, f32[1,224]{1,0:T(1,128)S(1)}) %tuple.68, (pred[]{:T(512)}, f32[1,2048]{1,0:T(1,128)S(1)}, bf16[1,2048,2048]{2,1,0:T(8,128)(2,1)}, ...), branch_computations={%region_5.5_spmd, %region_6.7_spmd} | conditional | flops 268959840 | bytes 9987569 | solution.py:95
  56.2 6.5 %conditional.3 = (f32[1,224,2048]{2,1,0:T(8,128)S(1)}, f32[1,224]{1,0:T(1,128)S(1)}, bf16[32,2048]{1,0:T(8,128)(2,1)S(1)}) conditional(s32[]{:T(128)} %convert_element_type.47, (f32[1,224,2048]{2,1,0:T(8,128)S(1)}, f32[1,224]{1,0:T(1,128)S(1)}) %tuple.68, (pred[]{:T(512)}, f32[1,2048]{1,0:T(1,128)S(1)}, bf16[1,2048,2048]{2,1,0:T(8,128)(2,1)}, ...), branch_computations={%region_5.5_spmd, %region_6.7_spmd} | conditional | flops 268959840 | bytes 9987569 | solution.py:95
  67.2 6.5 %conditional.3 = (f32[1,224,2048]{2,1,0:T(8,128)S(1)}, f32[1,224]{1,0:T(1,128)S(1)}, bf16[32,2048]{1,0:T(8,128)(2,1)S(1)}) conditional(s32[]{:T(128)} %convert_element_type.47, (f32[1,224,2048]{2,1,0:T(8,128)S(1)}, f32[1,224]{1,0:T(1,128)S(1)}) %tuple.68, (pred[]{:T(512)}, f32[1,2048]{1,0:T(1,128)S(1)}, bf16[1,2048,2048]{2,1,0:T(8,128)(2,1)}, ...), branch_computations={%region_5.5_spmd, %region_6.7_spmd} | conditional | flops 268959840 | bytes 9987569 | solution.py:95
  80.6 6.4 %conditional.3 = (f32[1,224,2048]{2,1,0:T(8,128)S(1)}, f32[1,224]{1,0:T(1,128)S(1)}, bf16[32,2048]{1,0:T(8,128)(2,1)S(1)}) conditional(s32[]{:T(128)} %convert_element_type.47, (f32[1,224,2048]{2,1,0:T(8,128)S(1)}, f32[1,224]{1,0:T(1,128)S(1)}) %tuple.68, (pred[]{:T(512)}, f32[1,2048]{1,0:T(1,128)S(1)}, bf16[1,2048,2048]{2,1,0:T(8,128)(2,1)}, ...), branch_computations={%region_5.5_spmd, %region_6.7_spmd} | conditional | flops 268959840 | bytes 9987569 | solution.py:95
  94.1 6.5 %conditional.3 = (f32[1,224,2048]{2,1,0:T(8,128)S(1)}, f32[1,224]{1,0:T(1,128)S(1)}, bf16[32,2048]{1,0:T(8,128)(2,1)S(1)}) conditional(s32[]{:T(128)} %convert_element_type.47, (f32[1,224,2048]{2,1,0:T(8,128)S(1)}, f32[1,224]{1,0:T(1,128)S(1)}) %tuple.68, (pred[]{:T(512)}, f32[1,2048]{1,0:T(1,128)S(1)}, bf16[1,2048,2048]{2,1,0:T(8,128)(2,1)}, ...), branch_computations={%region_5.5_spmd, %region_6.7_spmd} | conditional | flops 268959840 | bytes 9987569 | solution.py:95
  107.5 6.5 %conditional.3 = (f32[1,224,2048]{2,1,0:T(8,128)S(1)}, f32[1,224]{1,0:T(1,128)S(1)}, bf16[32,2048]{1,0:T(8,128)(2,1)S(1)}) conditional(s32[]{:T(128)} %convert_element_type.47, (f32[1,224,2048]{2,1,0:T(8,128)S(1)}, f32[1,224]{1,0:T(1,128)S(1)}) %tuple.68, (pred[]{:T(512)}, f32[1,2048]{1,0:T(1,128)S(1)}, bf16[1,2048,2048]{2,1,0:T(8,128)(2,1)}, ...), branch_computations={%region_5.5_spmd, %region_6.7_spmd} | conditional | flops 268959840 | bytes 9987569 | solution.py:95
  121.1 11.7 %collective-permute-start = (bf16[32,2048]{1,0:T(8,128)(2,1)S(1)}, bf16[32,2048]{1,0:T(8,128)(2,1)S(1)}, u32[]{:S(2)}, u32[]{:S(2)}) collective-permute-start(bf16[32,2048]{1,0:T(8,128)(2,1)S(1)} %get-tuple-element.433), channel_id=1, source_target_pairs={{0,1},{1,2},{2,3},{3,4},{4,5},{5,6},{6,7},{7,8},{8,9},{9,10},{10,1... | collective-permute-start | bytes 393224 | tf_op jit(solution)/shard_map/while/body/eval_jaxpr/ppermute | solution.py:14
  141.5 11.8 %collective-permute-start = (bf16[32,2048]{1,0:T(8,128)(2,1)S(1)}, bf16[32,2048]{1,0:T(8,128)(2,1)S(1)}, u32[]{:S(2)}, u32[]{:S(2)}) collective-permute-start(bf16[32,2048]{1,0:T(8,128)(2,1)S(1)} %get-tuple-element.433), channel_id=1, source_target_pairs={{0,1},{1,2},{2,3},{3,4},{4,5},{5,6},{6,7},{7,8},{8,9},{9,10},{10,1... | collective-permute-start | bytes 393224 | tf_op jit(solution)/shard_map/while/body/eval_jaxpr/ppermute | solution.py:14
  162.0 7.3 %collective-permute-start = (bf16[32,2048]{1,0:T(8,128)(2,1)S(1)}, bf16[32,2048]{1,0:T(8,128)(2,1)S(1)}, u32[]{:S(2)}, u32[]{:S(2)}) collective-permute-start(bf16[32,2048]{1,0:T(8,128)(2,1)S(1)} %get-tuple-element.433), channel_id=1, source_target_pairs={{0,1},{1,2},{2,3},{3,4},{4,5},{5,6},{6,7},{7,8},{8,9},{9,10},{10,1... | collective-permute-start | bytes 393224 | tf_op jit(solution)/shard_map/while/body/eval_jaxpr/ppermute | solution.py:14
  170.9 6.2 %collective-permute-start = (bf16[32,2048]{1,0:T(8,128)(2,1)S(1)}, bf16[32,2048]{1,0:T(8,128)(2,1)S(1)}, u32[]{:S(2)}, u32[]{:S(2)}) collective-permute-start(bf16[32,2048]{1,0:T(8,128)(2,1)S(1)} %get-tuple-element.433), channel_id=1, source_target_pairs={{0,1},{1,2},{2,3},{3,4},{4,5},{5,6},{6,7},{7,8},{8,9},{9,10},{10,1... | collective-permute-start | bytes 393224 | tf_op jit(solution)/shard_map/while/body/eval_jaxpr/ppermute | solution.py:14
  178.8 12.7 %collective-permute-start = (bf16[32,2048]{1,0:T(8,128)(2,1)S(1)}, bf16[32,2048]{1,0:T(8,128)(2,1)S(1)}, u32[]{:S(2)}, u32[]{:S(2)}) collective-permute-start(bf16[32,2048]{1,0:T(8,128)(2,1)S(1)} %get-tuple-element.433), channel_id=1, source_target_pairs={{0,1},{1,2},{2,3},{3,4},{4,5},{5,6},{6,7},{7,8},{8,9},{9,10},{10,1... | collective-permute-start | bytes 393224 | tf_op jit(solution)/shard_map/while/body/eval_jaxpr/ppermute | solution.py:14
  193.2 6.2 %collective-permute-start = (bf16[32,2048]{1,0:T(8,128)(2,1)S(1)}, bf16[32,2048]{1,0:T(8,128)(2,1)S(1)}, u32[]{:S(2)}, u32[]{:S(2)}) collective-permute-start(bf16[32,2048]{1,0:T(8,128)(2,1)S(1)} %get-tuple-element.433), channel_id=1, source_target_pairs={{0,1},{1,2},{2,3},{3,4},{4,5},{5,6},{6,7},{7,8},{8,9},{9,10},{10,1... | collective-permute-start | bytes 393224 | tf_op jit(solution)/shard_map/while/body/eval_jaxpr/ppermute | solution.py:14
  216.9 6.7 %collective-permute-start = (bf16[32,2048]{1,0:T(8,128)(2,1)S(1)}, bf16[32,2048]{1,0:T(8,128)(2,1)S(1)}, u32[]{:S(2)}, u32[]{:S(2)}) collective-permute-start(bf16[32,2048]{1,0:T(8,128)(2,1)S(1)} %get-tuple-element.433), channel_id=1, source_target_pairs={{0,1},{1,2},{2,3},{3,4},{4,5},{5,6},{6,7},{7,8},{8,9},{9,10},{10,1... | collective-permute-start | bytes 393224 | tf_op jit(solution)/shard_map/while/body/eval_jaxpr/ppermute | solution.py:14
  225.2 6.2 %collective-permute-start = (bf16[32,2048]{1,0:T(8,128)(2,1)S(1)}, bf16[32,2048]{1,0:T(8,128)(2,1)S(1)}, u32[]{:S(2)}, u32[]{:S(2)}) collective-permute-start(bf16[32,2048]{1,0:T(8,128)(2,1)S(1)} %get-tuple-element.433), channel_id=1, source_target_pairs={{0,1},{1,2},{2,3},{3,4},{4,5},{5,6},{6,7},{7,8},{8,9},{9,10},{10,1... | collective-permute-start | bytes 393224 | tf_op jit(solution)/shard_map/while/body/eval_jaxpr/ppermute | solution.py:14
  233.2 6.2 %collective-permute-start = (bf16[32,2048]{1,0:T(8,128)(2,1)S(1)}, bf16[32,2048]{1,0:T(8,128)(2,1)S(1)}, u32[]{:S(2)}, u32[]{:S(2)}) collective-permute-start(bf16[32,2048]{1,0:T(8,128)(2,1)S(1)} %get-tuple-element.433), channel_id=1, source_target_pairs={{0,1},{1,2},{2,3},{3,4},{4,5},{5,6},{6,7},{7,8},{8,9},{9,10},{10,1... | collective-permute-start | bytes 393224 | tf_op jit(solution)/shard_map/while/body/eval_jaxpr/ppermute | solution.py:14
  249.0 7.6 %collective-permute-start = (bf16[32,2048]{1,0:T(8,128)(2,1)S(1)}, bf16[32,2048]{1,0:T(8,128)(2,1)S(1)}, u32[]{:S(2)}, u32[]{:S(2)}) collective-permute-start(bf16[32,2048]{1,0:T(8,128)(2,1)S(1)} %get-tuple-element.433), channel_id=1, source_target_pairs={{0,1},{1,2},{2,3},{3,4},{4,5},{5,6},{6,7},{7,8},{8,9},{9,10},{10,1... | collective-permute-start | bytes 393224 | tf_op jit(solution)/shard_map/while/body/eval_jaxpr/ppermute | solution.py:14
  257.6 76.6 %psum.7 = f32[224]{0:T(256)S(1)} all-reduce(f32[224]{0:T(256)S(1)} %bitcast.57), channel_id=1, replica_groups=mesh['groups'=2,'tm'=16] {'tm'}, use_global_device_ids=true, to_apply=%region_9.10 | all-reduce | flops 224 | bytes 1792 | tf_op jit(solution)/shard_map/psum | solution.py:106
  (140 shorter events, 147.1 us)
Async XLA Ops:
  0.6 4.2 %collective-permute-start.1 = (f32[64,2048]{1,0:T(8,128)}, f32[64,2048]{1,0:T(8,128)S(1)}, u32[]{:S(2)}, u32[]{:S(2)}) collective-permute-start(f32[64,2048]{1,0:T(8,128)} %bitcast.54), channel_id=1, source_target_pairs={{0,1},{1,2},{2,3},{3,4},{4,5},{5,6},{6,7},{7,8},{8,9},{9,10},{10,1... | collective-permute-start | bytes 1572872 | tf_op jit(solution)/shard_map/ppermute | solution.py:14
  38.5 3.7 %collective-permute-start = (bf16[32,2048]{1,0:T(8,128)(2,1)S(1)}, bf16[32,2048]{1,0:T(8,128)(2,1)S(1)}, u32[]{:S(2)}, u32[]{:S(2)}) collective-permute-start(bf16[32,2048]{1,0:T(8,128)(2,1)S(1)} %get-tuple-element.433), channel_id=1, source_target_pairs={{0,1},{1,2},{2,3},{3,4},{4,5},{5,6},{6,7},{7,8},{8,9},{9,10},{10,1... | collective-permute-start | bytes 393224 | tf_op jit(solution)/shard_map/while/body/eval_jaxpr/ppermute | solution.py:14
  49.4 6.1 %collective-permute-start = (bf16[32,2048]{1,0:T(8,128)(2,1)S(1)}, bf16[32,2048]{1,0:T(8,128)(2,1)S(1)}, u32[]{:S(2)}, u32[]{:S(2)}) collective-permute-start(bf16[32,2048]{1,0:T(8,128)(2,1)S(1)} %get-tuple-element.433), channel_id=1, source_target_pairs={{0,1},{1,2},{2,3},{3,4},{4,5},{5,6},{6,7},{7,8},{8,9},{9,10},{10,1... | collective-permute-start | bytes 393224 | tf_op jit(solution)/shard_map/while/body/eval_jaxpr/ppermute | solution.py:14
  62.7 3.9 %collective-permute-start = (bf16[32,2048]{1,0:T(8,128)(2,1)S(1)}, bf16[32,2048]{1,0:T(8,128)(2,1)S(1)}, u32[]{:S(2)}, u32[]{:S(2)}) collective-permute-start(bf16[32,2048]{1,0:T(8,128)(2,1)S(1)} %get-tuple-element.433), channel_id=1, source_target_pairs={{0,1},{1,2},{2,3},{3,4},{4,5},{5,6},{6,7},{7,8},{8,9},{9,10},{10,1... | collective-permute-start | bytes 393224 | tf_op jit(solution)/shard_map/while/body/eval_jaxpr/ppermute | solution.py:14
  73.8 6.2 %collective-permute-start = (bf16[32,2048]{1,0:T(8,128)(2,1)S(1)}, bf16[32,2048]{1,0:T(8,128)(2,1)S(1)}, u32[]{:S(2)}, u32[]{:S(2)}) collective-permute-start(bf16[32,2048]{1,0:T(8,128)(2,1)S(1)} %get-tuple-element.433), channel_id=1, source_target_pairs={{0,1},{1,2},{2,3},{3,4},{4,5},{5,6},{6,7},{7,8},{8,9},{9,10},{10,1... | collective-permute-start | bytes 393224 | tf_op jit(solution)/shard_map/while/body/eval_jaxpr/ppermute | solution.py:14
  87.1 6.4 %collective-permute-start = (bf16[32,2048]{1,0:T(8,128)(2,1)S(1)}, bf16[32,2048]{1,0:T(8,128)(2,1)S(1)}, u32[]{:S(2)}, u32[]{:S(2)}) collective-permute-start(bf16[32,2048]{1,0:T(8,128)(2,1)S(1)} %get-tuple-element.433), channel_id=1, source_target_pairs={{0,1},{1,2},{2,3},{3,4},{4,5},{5,6},{6,7},{7,8},{8,9},{9,10},{10,1... | collective-permute-start | bytes 393224 | tf_op jit(solution)/shard_map/while/body/eval_jaxpr/ppermute | solution.py:14
  100.6 6.2 %collective-permute-start = (bf16[32,2048]{1,0:T(8,128)(2,1)S(1)}, bf16[32,2048]{1,0:T(8,128)(2,1)S(1)}, u32[]{:S(2)}, u32[]{:S(2)}) collective-permute-start(bf16[32,2048]{1,0:T(8,128)(2,1)S(1)} %get-tuple-element.433), channel_id=1, source_target_pairs={{0,1},{1,2},{2,3},{3,4},{4,5},{5,6},{6,7},{7,8},{8,9},{9,10},{10,1... | collective-permute-start | bytes 393224 | tf_op jit(solution)/shard_map/while/body/eval_jaxpr/ppermute | solution.py:14
  114.0 6.4 %collective-permute-start = (bf16[32,2048]{1,0:T(8,128)(2,1)S(1)}, bf16[32,2048]{1,0:T(8,128)(2,1)S(1)}, u32[]{:S(2)}, u32[]{:S(2)}) collective-permute-start(bf16[32,2048]{1,0:T(8,128)(2,1)S(1)} %get-tuple-element.433), channel_id=1, source_target_pairs={{0,1},{1,2},{2,3},{3,4},{4,5},{5,6},{6,7},{7,8},{8,9},{9,10},{10,1... | collective-permute-start | bytes 393224 | tf_op jit(solution)/shard_map/while/body/eval_jaxpr/ppermute | solution.py:14
  121.1 12.7 %collective-permute-start = (bf16[32,2048]{1,0:T(8,128)(2,1)S(1)}, bf16[32,2048]{1,0:T(8,128)(2,1)S(1)}, u32[]{:S(2)}, u32[]{:S(2)}) collective-permute-start(bf16[32,2048]{1,0:T(8,128)(2,1)S(1)} %get-tuple-element.433), channel_id=1, source_target_pairs={{0,1},{1,2},{2,3},{3,4},{4,5},{5,6},{6,7},{7,8},{8,9},{9,10},{10,1... | collective-permute-start | bytes 393224 | tf_op jit(solution)/shard_map/while/body/eval_jaxpr/ppermute | solution.py:14
  134.5 6.3 %collective-permute-start = (bf16[32,2048]{1,0:T(8,128)(2,1)S(1)}, bf16[32,2048]{1,0:T(8,128)(2,1)S(1)}, u32[]{:S(2)}, u32[]{:S(2)}) collective-permute-start(bf16[32,2048]{1,0:T(8,128)(2,1)S(1)} %get-tuple-element.433), channel_id=1, source_target_pairs={{0,1},{1,2},{2,3},{3,4},{4,5},{5,6},{6,7},{7,8},{8,9},{9,10},{10,1... | collective-permute-start | bytes 393224 | tf_op jit(solution)/shard_map/while/body/eval_jaxpr/ppermute | solution.py:14
  141.5 12.8 %collective-permute-start = (bf16[32,2048]{1,0:T(8,128)(2,1)S(1)}, bf16[32,2048]{1,0:T(8,128)(2,1)S(1)}, u32[]{:S(2)}, u32[]{:S(2)}) collective-permute-start(bf16[32,2048]{1,0:T(8,128)(2,1)S(1)} %get-tuple-element.433), channel_id=1, source_target_pairs={{0,1},{1,2},{2,3},{3,4},{4,5},{5,6},{6,7},{7,8},{8,9},{9,10},{10,1... | collective-permute-start | bytes 393224 | tf_op jit(solution)/shard_map/while/body/eval_jaxpr/ppermute | solution.py:14
  155.0 6.3 %collective-permute-start = (bf16[32,2048]{1,0:T(8,128)(2,1)S(1)}, bf16[32,2048]{1,0:T(8,128)(2,1)S(1)}, u32[]{:S(2)}, u32[]{:S(2)}) collective-permute-start(bf16[32,2048]{1,0:T(8,128)(2,1)S(1)} %get-tuple-element.433), channel_id=1, source_target_pairs={{0,1},{1,2},{2,3},{3,4},{4,5},{5,6},{6,7},{7,8},{8,9},{9,10},{10,1... | collective-permute-start | bytes 393224 | tf_op jit(solution)/shard_map/while/body/eval_jaxpr/ppermute | solution.py:14
  162.0 8.2 %collective-permute-start = (bf16[32,2048]{1,0:T(8,128)(2,1)S(1)}, bf16[32,2048]{1,0:T(8,128)(2,1)S(1)}, u32[]{:S(2)}, u32[]{:S(2)}) collective-permute-start(bf16[32,2048]{1,0:T(8,128)(2,1)S(1)} %get-tuple-element.433), channel_id=1, source_target_pairs={{0,1},{1,2},{2,3},{3,4},{4,5},{5,6},{6,7},{7,8},{8,9},{9,10},{10,1... | collective-permute-start | bytes 393224 | tf_op jit(solution)/shard_map/while/body/eval_jaxpr/ppermute | solution.py:14
  170.9 7.2 %collective-permute-start = (bf16[32,2048]{1,0:T(8,128)(2,1)S(1)}, bf16[32,2048]{1,0:T(8,128)(2,1)S(1)}, u32[]{:S(2)}, u32[]{:S(2)}) collective-permute-start(bf16[32,2048]{1,0:T(8,128)(2,1)S(1)} %get-tuple-element.433), channel_id=1, source_target_pairs={{0,1},{1,2},{2,3},{3,4},{4,5},{5,6},{6,7},{7,8},{8,9},{9,10},{10,1... | collective-permute-start | bytes 393224 | tf_op jit(solution)/shard_map/while/body/eval_jaxpr/ppermute | solution.py:14
  178.8 13.7 %collective-permute-start = (bf16[32,2048]{1,0:T(8,128)(2,1)S(1)}, bf16[32,2048]{1,0:T(8,128)(2,1)S(1)}, u32[]{:S(2)}, u32[]{:S(2)}) collective-permute-start(bf16[32,2048]{1,0:T(8,128)(2,1)S(1)} %get-tuple-element.433), channel_id=1, source_target_pairs={{0,1},{1,2},{2,3},{3,4},{4,5},{5,6},{6,7},{7,8},{8,9},{9,10},{10,1... | collective-permute-start | bytes 393224 | tf_op jit(solution)/shard_map/while/body/eval_jaxpr/ppermute | solution.py:14
  193.2 7.2 %collective-permute-start = (bf16[32,2048]{1,0:T(8,128)(2,1)S(1)}, bf16[32,2048]{1,0:T(8,128)(2,1)S(1)}, u32[]{:S(2)}, u32[]{:S(2)}) collective-permute-start(bf16[32,2048]{1,0:T(8,128)(2,1)S(1)} %get-tuple-element.433), channel_id=1, source_target_pairs={{0,1},{1,2},{2,3},{3,4},{4,5},{5,6},{6,7},{7,8},{8,9},{9,10},{10,1... | collective-permute-start | bytes 393224 | tf_op jit(solution)/shard_map/while/body/eval_jaxpr/ppermute | solution.py:14
  201.1 7.2 %collective-permute-start = (bf16[32,2048]{1,0:T(8,128)(2,1)S(1)}, bf16[32,2048]{1,0:T(8,128)(2,1)S(1)}, u32[]{:S(2)}, u32[]{:S(2)}) collective-permute-start(bf16[32,2048]{1,0:T(8,128)(2,1)S(1)} %get-tuple-element.433), channel_id=1, source_target_pairs={{0,1},{1,2},{2,3},{3,4},{4,5},{5,6},{6,7},{7,8},{8,9},{9,10},{10,1... | collective-permute-start | bytes 393224 | tf_op jit(solution)/shard_map/while/body/eval_jaxpr/ppermute | solution.py:14
  209.0 7.2 %collective-permute-start = (bf16[32,2048]{1,0:T(8,128)(2,1)S(1)}, bf16[32,2048]{1,0:T(8,128)(2,1)S(1)}, u32[]{:S(2)}, u32[]{:S(2)}) collective-permute-start(bf16[32,2048]{1,0:T(8,128)(2,1)S(1)} %get-tuple-element.433), channel_id=1, source_target_pairs={{0,1},{1,2},{2,3},{3,4},{4,5},{5,6},{6,7},{7,8},{8,9},{9,10},{10,1... | collective-permute-start | bytes 393224 | tf_op jit(solution)/shard_map/while/body/eval_jaxpr/ppermute | solution.py:14
  216.9 7.6 %collective-permute-start = (bf16[32,2048]{1,0:T(8,128)(2,1)S(1)}, bf16[32,2048]{1,0:T(8,128)(2,1)S(1)}, u32[]{:S(2)}, u32[]{:S(2)}) collective-permute-start(bf16[32,2048]{1,0:T(8,128)(2,1)S(1)} %get-tuple-element.433), channel_id=1, source_target_pairs={{0,1},{1,2},{2,3},{3,4},{4,5},{5,6},{6,7},{7,8},{8,9},{9,10},{10,1... | collective-permute-start | bytes 393224 | tf_op jit(solution)/shard_map/while/body/eval_jaxpr/ppermute | solution.py:14
  225.2 7.2 %collective-permute-start = (bf16[32,2048]{1,0:T(8,128)(2,1)S(1)}, bf16[32,2048]{1,0:T(8,128)(2,1)S(1)}, u32[]{:S(2)}, u32[]{:S(2)}) collective-permute-start(bf16[32,2048]{1,0:T(8,128)(2,1)S(1)} %get-tuple-element.433), channel_id=1, source_target_pairs={{0,1},{1,2},{2,3},{3,4},{4,5},{5,6},{6,7},{7,8},{8,9},{9,10},{10,1... | collective-permute-start | bytes 393224 | tf_op jit(solution)/shard_map/while/body/eval_jaxpr/ppermute | solution.py:14
  233.2 7.2 %collective-permute-start = (bf16[32,2048]{1,0:T(8,128)(2,1)S(1)}, bf16[32,2048]{1,0:T(8,128)(2,1)S(1)}, u32[]{:S(2)}, u32[]{:S(2)}) collective-permute-start(bf16[32,2048]{1,0:T(8,128)(2,1)S(1)} %get-tuple-element.433), channel_id=1, source_target_pairs={{0,1},{1,2},{2,3},{3,4},{4,5},{5,6},{6,7},{7,8},{8,9},{9,10},{10,1... | collective-permute-start | bytes 393224 | tf_op jit(solution)/shard_map/while/body/eval_jaxpr/ppermute | solution.py:14
  241.1 7.2 %collective-permute-start = (bf16[32,2048]{1,0:T(8,128)(2,1)S(1)}, bf16[32,2048]{1,0:T(8,128)(2,1)S(1)}, u32[]{:S(2)}, u32[]{:S(2)}) collective-permute-start(bf16[32,2048]{1,0:T(8,128)(2,1)S(1)} %get-tuple-element.433), channel_id=1, source_target_pairs={{0,1},{1,2},{2,3},{3,4},{4,5},{5,6},{6,7},{7,8},{8,9},{9,10},{10,1... | collective-permute-start | bytes 393224 | tf_op jit(solution)/shard_map/while/body/eval_jaxpr/ppermute | solution.py:14
  249.0 8.6 %collective-permute-start = (bf16[32,2048]{1,0:T(8,128)(2,1)S(1)}, bf16[32,2048]{1,0:T(8,128)(2,1)S(1)}, u32[]{:S(2)}, u32[]{:S(2)}) collective-permute-start(bf16[32,2048]{1,0:T(8,128)(2,1)S(1)} %get-tuple-element.433), channel_id=1, source_target_pairs={{0,1},{1,2},{2,3},{3,4},{4,5},{5,6},{6,7},{7,8},{8,9},{9,10},{10,1... | collective-permute-start | bytes 393224 | tf_op jit(solution)/shard_map/while/body/eval_jaxpr/ppermute | solution.py:14
  257.5 77.2 %copy-start = (f32[1,224,2048]{2,1,0:T(8,128)}, f32[1,224,2048]{2,1,0:T(8,128)S(1)}, u32[]{:S(2)}) copy-start(f32[1,224,2048]{2,1,0:T(8,128)S(1)} %get-tuple-element.273) | copy-start | bytes 5505028
where the time goes:
time: 336 us; the launch traced here: 335 us
  starting transfers between devices  146 us (43%)
  blocking collectives  76.6 us (23%)
  matrix products  61.3 us (18%)
  other arithmetic  24.4 us (7%)
  waiting for transfers between devices  21.1 us (6%)
    ppermute x23, starting transfers between devices, shifted(): lax.ppermute(value, axis, [(source, source + steps) for source in range(i...  146 us
    psum x1, blocking collectives, per_device(): log_scale = lax.psum(local_log, 'tm') / (tm_count * local_slices - 1)  76.6 us
    dot_general x7, matrix products, push_forward(): jnp.dot(weighted, kernel, preferred_element_type=jnp.float32)  35.2 us
    dot_general x4, matrix products, one_block(): lax.dot_general(segment, target, (((0,), (0,)), ((), ())), precision=lax....  26.1 us
    ppermute x23, waiting for transfers between devices, shifted(): lax.ppermute(value, axis, [(source, source + steps) for source in range(i...  21.1 us
    convert_element_type x22, other arithmetic, per_device(): (jnp.arange(point_count, dtype=jnp.int32)[None, :] < supports[:, None]).a...  14.4 us
    convert_element_type x7, other arithmetic, section(): outgoing = (message * block_pot[local_slices - 1]).astype(jnp.bfloat16)  7.46 us
  transfers between devices with their start and end apart: 23, of which 22 were waited for; matrix products, arithmetic and copies ran while one was open for 0% of the time, Pallas kernels for 0%

commit v1 on v0

--- a/solution.py
+++ b/solution.py
@@ -103,7 +103,7 @@
     )
     unused, messages, log_parts = lax.fori_loop(0, phase_count, advance, initial)
     local_log = jnp.sum(log_parts, axis=0)
-    log_scale = lax.psum(local_log, "tm") / (tm_count * local_slices - 1)
+    log_scale = jnp.sum(lax.all_gather(local_log, "tm"), axis=0) / (tm_count * local_slices - 1)
     return (messages, log_scale)
 
 

time: 336 us -> 324 us (0.964)
  blocking collectives: 76.6 us -> 64.3 us
    psum x1 -> x0, blocking collectives: 76.6 us -> none  [per_device(): log_scale = lax.psum(local_log, 'tm') / (tm_count * local_slices - 1)]
    all_gather x0 -> x1, blocking collectives: none -> 64.3 us  [per_device(): lax.all_gather(local_log, 'tm')]
where the time goes in v1:
time: 324 us; the launch traced here: 322 us
  starting transfers between devices  146 us (45%)
  blocking collectives  64.3 us (20%)
  matrix products  61.3 us (19%)
  other arithmetic  24.5 us (8%)
  waiting for transfers between devices  21.1 us (7%)
    ppermute x23, starting transfers between devices, shifted(): lax.ppermute(value, axis, [(source, source + steps) for source in range(i...  146 us
    all_gather x1, blocking collectives, per_device(): lax.all_gather(local_log, 'tm')  64.3 us
    dot_general x7, matrix products, push_forward(): jnp.dot(weighted, kernel, preferred_element_type=jnp.float32)  35.2 us
    dot_general x4, matrix products, one_block(): lax.dot_general(segment, target, (((0,), (0,)), ((), ())), precision=lax....  26.1 us
    ppermute x23, waiting for transfers between devices, shifted(): lax.ppermute(value, axis, [(source, source + steps) for source in range(i...  21.1 us
    convert_element_type x22, other arithmetic, per_device(): (jnp.arange(point_count, dtype=jnp.int32)[None, :] < supports[:, None]).a...  14.4 us
    convert_element_type x7, other arithmetic, section(): outgoing = (message * block_pot[local_slices - 1]).astype(jnp.bfloat16)  7.46 us
  transfers between devices with their start and end apart: 23, of which 22 were waited for; matrix products, arithmetic and copies ran while one was open for 0% of the time, Pallas kernels for 0%

profile of v1, /device:TPU:0, one launch (start us, length us, event | category | flops | bytes accessed | tf_op | source)
XLA Modules:
  0.0 322.5 jit_solution(1200826836535629276)
XLA Ops:
  4.9 26.2 %while.35 = (s32[]{:T(128)}, bf16[4,512,2048]{2,1,0:T(8,128)(2,1)}, f32[2048]{0:T(1024)S(1)}, f32[4,64,512]{2,1,0:T(8,128)S(1)}, f32[64,2048]{1,0:T(8,128)}, /*index=5*/s32[]{:T(128)}) while((s32[]{:T(128)}, bf16[4,512,2048]{2,1,0:T(8,128)(2,1)}, f32[2048]{0:T(1024)S(1)}, f32[4,64,512]{2,1,0:T(8,128)S(1)}, f32[64,2048]{1,0:T(8,128)}, ...), condition=%wide.region_3.0_spmd, body=%wide.region_1.3_spmd.sunk | while | flops 810614784 | bytes 2901065 | solution.py:40
  4.9 6.5 %fusion.26 = bf16[4,512,2048]{2,1,0:T(8,128)(2,1)} fusion(bf16[4,512,2048]{2,1,0:T(8,128)(2,1)} %get-tuple-element.449, s32[]{:T(128)} %get-tuple-element.448, f32[64,2048]{1,0:T(8,128)} %get-tuple-element.458, f32[512]{0:T(512)S(1)} %broadcast_multiply_fusion.3, f32[2048]{0:T(1024)S(1)} %get-tuple-element.456, f32[4,64,512]{2,1,0:T(8,128)S(1)} %get-tuple-element.457), kind=kOutput, calls=%fused_computation.3.clone.1 | convolution fusion | flops 810549248 | bytes 2763776 | tf_op jit(solution)/shard_map/while/body/eval_jaxpr/while/body/eval_jaxpr/dot_general | solution.py:27
  11.5 6.5 %fusion.26 = bf16[4,512,2048]{2,1,0:T(8,128)(2,1)} fusion(bf16[4,512,2048]{2,1,0:T(8,128)(2,1)} %get-tuple-element.449, s32[]{:T(128)} %get-tuple-element.448, f32[64,2048]{1,0:T(8,128)} %get-tuple-element.458, f32[512]{0:T(512)S(1)} %broadcast_multiply_fusion.3, f32[2048]{0:T(1024)S(1)} %get-tuple-element.456, f32[4,64,512]{2,1,0:T(8,128)S(1)} %get-tuple-element.457), kind=kOutput, calls=%fused_computation.3.clone.1 | convolution fusion | flops 810549248 | bytes 2763776 | tf_op jit(solution)/shard_map/while/body/eval_jaxpr/while/body/eval_jaxpr/dot_general | solution.py:27
  18.1 6.5 %fusion.26 = bf16[4,512,2048]{2,1,0:T(8,128)(2,1)} fusion(bf16[4,512,2048]{2,1,0:T(8,128)(2,1)} %get-tuple-element.449, s32[]{:T(128)} %get-tuple-element.448, f32[64,2048]{1,0:T(8,128)} %get-tuple-element.458, f32[512]{0:T(512)S(1)} %broadcast_multiply_fusion.3, f32[2048]{0:T(1024)S(1)} %get-tuple-element.456, f32[4,64,512]{2,1,0:T(8,128)S(1)} %get-tuple-element.457), kind=kOutput, calls=%fused_computation.3.clone.1 | convolution fusion | flops 810549248 | bytes 2763776 | tf_op jit(solution)/shard_map/while/body/eval_jaxpr/while/body/eval_jaxpr/dot_general | solution.py:27
  24.6 6.5 %fusion.26 = bf16[4,512,2048]{2,1,0:T(8,128)(2,1)} fusion(bf16[4,512,2048]{2,1,0:T(8,128)(2,1)} %get-tuple-element.449, s32[]{:T(128)} %get-tuple-element.448, f32[64,2048]{1,0:T(8,128)} %get-tuple-element.458, f32[512]{0:T(512)S(1)} %broadcast_multiply_fusion.3, f32[2048]{0:T(1024)S(1)} %get-tuple-element.456, f32[4,64,512]{2,1,0:T(8,128)S(1)} %get-tuple-element.457), kind=kOutput, calls=%fused_computation.3.clone.1 | convolution fusion | flops 810549248 | bytes 2763776 | tf_op jit(solution)/shard_map/while/body/eval_jaxpr/while/body/eval_jaxpr/dot_general | solution.py:27
  31.4 226.2 %while.36 = (s32[]{:T(128)}, bf16[32,2048]{1,0:T(8,128)(2,1)S(1)}, f32[1,224,2048]{2,1,0:T(8,128)S(1)}, f32[1,224]{1,0:T(1,128)S(1)}, s32[]{:T(128)}, /*index=5*...) while((s32[]{:T(128)}, bf16[32,2048]{1,0:T(8,128)(2,1)S(1)}, ...), condition=%wide.region_8.9_spmd.clone, body=%wide.region_4.8_spmd.clone.sunk | while | flops 268963936 | bytes 10520344 | solution.py:104
  32.0 6.4 %conditional.3 = (f32[1,224,2048]{2,1,0:T(8,128)S(1)}, f32[1,224]{1,0:T(1,128)S(1)}, bf16[32,2048]{1,0:T(8,128)(2,1)S(1)}) conditional(s32[]{:T(128)} %convert_element_type.47, (f32[1,224,2048]{2,1,0:T(8,128)S(1)}, f32[1,224]{1,0:T(1,128)S(1)}) %tuple.68, (pred[]{:T(512)}, f32[1,2048]{1,0:T(1,128)S(1)}, bf16[1,2048,2048]{2,1,0:T(8,128)(2,1)}, ...), branch_computations={%region_5.5_spmd, %region_6.7_spmd} | conditional | flops 268959840 | bytes 9987569 | solution.py:95
  42.9 6.5 %conditional.3 = (f32[1,224,2048]{2,1,0:T(8,128)S(1)}, f32[1,224]{1,0:T(1,128)S(1)}, bf16[32,2048]{1,0:T(8,128)(2,1)S(1)}) conditional(s32[]{:T(128)} %convert_element_type.47, (f32[1,224,2048]{2,1,0:T(8,128)S(1)}, f32[1,224]{1,0:T(1,128)S(1)}) %tuple.68, (pred[]{:T(512)}, f32[1,2048]{1,0:T(1,128)S(1)}, bf16[1,2048,2048]{2,1,0:T(8,128)(2,1)}, ...), branch_computations={%region_5.5_spmd, %region_6.7_spmd} | conditional | flops 268959840 | bytes 9987569 | solution.py:95
  56.2 6.5 %conditional.3 = (f32[1,224,2048]{2,1,0:T(8,128)S(1)}, f32[1,224]{1,0:T(1,128)S(1)}, bf16[32,2048]{1,0:T(8,128)(2,1)S(1)}) conditional(s32[]{:T(128)} %convert_element_type.47, (f32[1,224,2048]{2,1,0:T(8,128)S(1)}, f32[1,224]{1,0:T(1,128)S(1)}) %tuple.68, (pred[]{:T(512)}, f32[1,2048]{1,0:T(1,128)S(1)}, bf16[1,2048,2048]{2,1,0:T(8,128)(2,1)}, ...), branch_computations={%region_5.5_spmd, %region_6.7_spmd} | conditional | flops 268959840 | bytes 9987569 | solution.py:95
  67.2 6.5 %conditional.3 = (f32[1,224,2048]{2,1,0:T(8,128)S(1)}, f32[1,224]{1,0:T(1,128)S(1)}, bf16[32,2048]{1,0:T(8,128)(2,1)S(1)}) conditional(s32[]{:T(128)} %convert_element_type.47, (f32[1,224,2048]{2,1,0:T(8,128)S(1)}, f32[1,224]{1,0:T(1,128)S(1)}) %tuple.68, (pred[]{:T(512)}, f32[1,2048]{1,0:T(1,128)S(1)}, bf16[1,2048,2048]{2,1,0:T(8,128)(2,1)}, ...), branch_computations={%region_5.5_spmd, %region_6.7_spmd} | conditional | flops 268959840 | bytes 9987569 | solution.py:95
  80.6 6.4 %conditional.3 = (f32[1,224,2048]{2,1,0:T(8,128)S(1)}, f32[1,224]{1,0:T(1,128)S(1)}, bf16[32,2048]{1,0:T(8,128)(2,1)S(1)}) conditional(s32[]{:T(128)} %convert_element_type.47, (f32[1,224,2048]{2,1,0:T(8,128)S(1)}, f32[1,224]{1,0:T(1,128)S(1)}) %tuple.68, (pred[]{:T(512)}, f32[1,2048]{1,0:T(1,128)S(1)}, bf16[1,2048,2048]{2,1,0:T(8,128)(2,1)}, ...), branch_computations={%region_5.5_spmd, %region_6.7_spmd} | conditional | flops 268959840 | bytes 9987569 | solution.py:95
  94.1 6.5 %conditional.3 = (f32[1,224,2048]{2,1,0:T(8,128)S(1)}, f32[1,224]{1,0:T(1,128)S(1)}, bf16[32,2048]{1,0:T(8,128)(2,1)S(1)}) conditional(s32[]{:T(128)} %convert_element_type.47, (f32[1,224,2048]{2,1,0:T(8,128)S(1)}, f32[1,224]{1,0:T(1,128)S(1)}) %tuple.68, (pred[]{:T(512)}, f32[1,2048]{1,0:T(1,128)S(1)}, bf16[1,2048,2048]{2,1,0:T(8,128)(2,1)}, ...), branch_computations={%region_5.5_spmd, %region_6.7_spmd} | conditional | flops 268959840 | bytes 9987569 | solution.py:95
  107.5 6.5 %conditional.3 = (f32[1,224,2048]{2,1,0:T(8,128)S(1)}, f32[1,224]{1,0:T(1,128)S(1)}, bf16[32,2048]{1,0:T(8,128)(2,1)S(1)}) conditional(s32[]{:T(128)} %convert_element_type.47, (f32[1,224,2048]{2,1,0:T(8,128)S(1)}, f32[1,224]{1,0:T(1,128)S(1)}) %tuple.68, (pred[]{:T(512)}, f32[1,2048]{1,0:T(1,128)S(1)}, bf16[1,2048,2048]{2,1,0:T(8,128)(2,1)}, ...), branch_computations={%region_5.5_spmd, %region_6.7_spmd} | conditional | flops 268959840 | bytes 9987569 | solution.py:95
  121.1 11.7 %collective-permute-start = (bf16[32,2048]{1,0:T(8,128)(2,1)S(1)}, bf16[32,2048]{1,0:T(8,128)(2,1)S(1)}, u32[]{:S(2)}, u32[]{:S(2)}) collective-permute-start(bf16[32,2048]{1,0:T(8,128)(2,1)S(1)} %get-tuple-element.433), channel_id=1, source_target_pairs={{0,1},{1,2},{2,3},{3,4},{4,5},{5,6},{6,7},{7,8},{8,9},{9,10},{10,1... | collective-permute-start | bytes 393224 | tf_op jit(solution)/shard_map/while/body/eval_jaxpr/ppermute | solution.py:14
  141.5 11.8 %collective-permute-start = (bf16[32,2048]{1,0:T(8,128)(2,1)S(1)}, bf16[32,2048]{1,0:T(8,128)(2,1)S(1)}, u32[]{:S(2)}, u32[]{:S(2)}) collective-permute-start(bf16[32,2048]{1,0:T(8,128)(2,1)S(1)} %get-tuple-element.433), channel_id=1, source_target_pairs={{0,1},{1,2},{2,3},{3,4},{4,5},{5,6},{6,7},{7,8},{8,9},{9,10},{10,1... | collective-permute-start | bytes 393224 | tf_op jit(solution)/shard_map/while/body/eval_jaxpr/ppermute | solution.py:14
  162.0 7.3 %collective-permute-start = (bf16[32,2048]{1,0:T(8,128)(2,1)S(1)}, bf16[32,2048]{1,0:T(8,128)(2,1)S(1)}, u32[]{:S(2)}, u32[]{:S(2)}) collective-permute-start(bf16[32,2048]{1,0:T(8,128)(2,1)S(1)} %get-tuple-element.433), channel_id=1, source_target_pairs={{0,1},{1,2},{2,3},{3,4},{4,5},{5,6},{6,7},{7,8},{8,9},{9,10},{10,1... | collective-permute-start | bytes 393224 | tf_op jit(solution)/shard_map/while/body/eval_jaxpr/ppermute | solution.py:14
  170.9 6.2 %collective-permute-start = (bf16[32,2048]{1,0:T(8,128)(2,1)S(1)}, bf16[32,2048]{1,0:T(8,128)(2,1)S(1)}, u32[]{:S(2)}, u32[]{:S(2)}) collective-permute-start(bf16[32,2048]{1,0:T(8,128)(2,1)S(1)} %get-tuple-element.433), channel_id=1, source_target_pairs={{0,1},{1,2},{2,3},{3,4},{4,5},{5,6},{6,7},{7,8},{8,9},{9,10},{10,1... | collective-permute-start | bytes 393224 | tf_op jit(solution)/shard_map/while/body/eval_jaxpr/ppermute | solution.py:14
  178.8 12.7 %collective-permute-start = (bf16[32,2048]{1,0:T(8,128)(2,1)S(1)}, bf16[32,2048]{1,0:T(8,128)(2,1)S(1)}, u32[]{:S(2)}, u32[]{:S(2)}) collective-permute-start(bf16[32,2048]{1,0:T(8,128)(2,1)S(1)} %get-tuple-element.433), channel_id=1, source_target_pairs={{0,1},{1,2},{2,3},{3,4},{4,5},{5,6},{6,7},{7,8},{8,9},{9,10},{10,1... | collective-permute-start | bytes 393224 | tf_op jit(solution)/shard_map/while/body/eval_jaxpr/ppermute | solution.py:14
  193.2 6.2 %collective-permute-start = (bf16[32,2048]{1,0:T(8,128)(2,1)S(1)}, bf16[32,2048]{1,0:T(8,128)(2,1)S(1)}, u32[]{:S(2)}, u32[]{:S(2)}) collective-permute-start(bf16[32,2048]{1,0:T(8,128)(2,1)S(1)} %get-tuple-element.433), channel_id=1, source_target_pairs={{0,1},{1,2},{2,3},{3,4},{4,5},{5,6},{6,7},{7,8},{8,9},{9,10},{10,1... | collective-permute-start | bytes 393224 | tf_op jit(solution)/shard_map/while/body/eval_jaxpr/ppermute | solution.py:14
  216.9 6.7 %collective-permute-start = (bf16[32,2048]{1,0:T(8,128)(2,1)S(1)}, bf16[32,2048]{1,0:T(8,128)(2,1)S(1)}, u32[]{:S(2)}, u32[]{:S(2)}) collective-permute-start(bf16[32,2048]{1,0:T(8,128)(2,1)S(1)} %get-tuple-element.433), channel_id=1, source_target_pairs={{0,1},{1,2},{2,3},{3,4},{4,5},{5,6},{6,7},{7,8},{8,9},{9,10},{10,1... | collective-permute-start | bytes 393224 | tf_op jit(solution)/shard_map/while/body/eval_jaxpr/ppermute | solution.py:14
  225.2 6.2 %collective-permute-start = (bf16[32,2048]{1,0:T(8,128)(2,1)S(1)}, bf16[32,2048]{1,0:T(8,128)(2,1)S(1)}, u32[]{:S(2)}, u32[]{:S(2)}) collective-permute-start(bf16[32,2048]{1,0:T(8,128)(2,1)S(1)} %get-tuple-element.433), channel_id=1, source_target_pairs={{0,1},{1,2},{2,3},{3,4},{4,5},{5,6},{6,7},{7,8},{8,9},{9,10},{10,1... | collective-permute-start | bytes 393224 | tf_op jit(solution)/shard_map/while/body/eval_jaxpr/ppermute | solution.py:14
  233.2 6.2 %collective-permute-start = (bf16[32,2048]{1,0:T(8,128)(2,1)S(1)}, bf16[32,2048]{1,0:T(8,128)(2,1)S(1)}, u32[]{:S(2)}, u32[]{:S(2)}) collective-permute-start(bf16[32,2048]{1,0:T(8,128)(2,1)S(1)} %get-tuple-element.433), channel_id=1, source_target_pairs={{0,1},{1,2},{2,3},{3,4},{4,5},{5,6},{6,7},{7,8},{8,9},{9,10},{10,1... | collective-permute-start | bytes 393224 | tf_op jit(solution)/shard_map/while/body/eval_jaxpr/ppermute | solution.py:14
  249.0 7.6 %collective-permute-start = (bf16[32,2048]{1,0:T(8,128)(2,1)S(1)}, bf16[32,2048]{1,0:T(8,128)(2,1)S(1)}, u32[]{:S(2)}, u32[]{:S(2)}) collective-permute-start(bf16[32,2048]{1,0:T(8,128)(2,1)S(1)} %get-tuple-element.433), channel_id=1, source_target_pairs={{0,1},{1,2},{2,3},{3,4},{4,5},{5,6},{6,7},{7,8},{8,9},{9,10},{10,1... | collective-permute-start | bytes 393224 | tf_op jit(solution)/shard_map/while/body/eval_jaxpr/ppermute | solution.py:14
  257.6 64.3 %all-gather = f32[16,1,224]{2,1,0:T(1,128)S(1)} all-gather(f32[1,1,224]{2,1,0:T(1,128)S(1)} %bitcast.57), channel_id=1, replica_groups=mesh['groups'=2,'tm'=16] {'tm'}, dimensions={0}, use_global_device_ids=true | all-gather | bytes 15232 | tf_op jit(solution)/shard_map/all_gather | solution.py:106
  (141 shorter events, 147.1 us)
Async XLA Ops:
  0.6 4.2 %collective-permute-start.1 = (f32[64,2048]{1,0:T(8,128)}, f32[64,2048]{1,0:T(8,128)S(1)}, u32[]{:S(2)}, u32[]{:S(2)}) collective-permute-start(f32[64,2048]{1,0:T(8,128)} %bitcast.54), channel_id=1, source_target_pairs={{0,1},{1,2},{2,3},{3,4},{4,5},{5,6},{6,7},{7,8},{8,9},{9,10},{10,1... | collective-permute-start | bytes 1572872 | tf_op jit(solution)/shard_map/ppermute | solution.py:14
  38.5 3.7 %collective-permute-start = (bf16[32,2048]{1,0:T(8,128)(2,1)S(1)}, bf16[32,2048]{1,0:T(8,128)(2,1)S(1)}, u32[]{:S(2)}, u32[]{:S(2)}) collective-permute-start(bf16[32,2048]{1,0:T(8,128)(2,1)S(1)} %get-tuple-element.433), channel_id=1, source_target_pairs={{0,1},{1,2},{2,3},{3,4},{4,5},{5,6},{6,7},{7,8},{8,9},{9,10},{10,1... | collective-permute-start | bytes 393224 | tf_op jit(solution)/shard_map/while/body/eval_jaxpr/ppermute | solution.py:14
  49.4 6.1 %collective-permute-start = (bf16[32,2048]{1,0:T(8,128)(2,1)S(1)}, bf16[32,2048]{1,0:T(8,128)(2,1)S(1)}, u32[]{:S(2)}, u32[]{:S(2)}) collective-permute-start(bf16[32,2048]{1,0:T(8,128)(2,1)S(1)} %get-tuple-element.433), channel_id=1, source_target_pairs={{0,1},{1,2},{2,3},{3,4},{4,5},{5,6},{6,7},{7,8},{8,9},{9,10},{10,1... | collective-permute-start | bytes 393224 | tf_op jit(solution)/shard_map/while/body/eval_jaxpr/ppermute | solution.py:14
  62.7 3.9 %collective-permute-start = (bf16[32,2048]{1,0:T(8,128)(2,1)S(1)}, bf16[32,2048]{1,0:T(8,128)(2,1)S(1)}, u32[]{:S(2)}, u32[]{:S(2)}) collective-permute-start(bf16[32,2048]{1,0:T(8,128)(2,1)S(1)} %get-tuple-element.433), channel_id=1, source_target_pairs={{0,1},{1,2},{2,3},{3,4},{4,5},{5,6},{6,7},{7,8},{8,9},{9,10},{10,1... | collective-permute-start | bytes 393224 | tf_op jit(solution)/shard_map/while/body/eval_jaxpr/ppermute | solution.py:14
  73.8 6.2 %collective-permute-start = (bf16[32,2048]{1,0:T(8,128)(2,1)S(1)}, bf16[32,2048]{1,0:T(8,128)(2,1)S(1)}, u32[]{:S(2)}, u32[]{:S(2)}) collective-permute-start(bf16[32,2048]{1,0:T(8,128)(2,1)S(1)} %get-tuple-element.433), channel_id=1, source_target_pairs={{0,1},{1,2},{2,3},{3,4},{4,5},{5,6},{6,7},{7,8},{8,9},{9,10},{10,1... | collective-permute-start | bytes 393224 | tf_op jit(solution)/shard_map/while/body/eval_jaxpr/ppermute | solution.py:14
  87.1 6.4 %collective-permute-start = (bf16[32,2048]{1,0:T(8,128)(2,1)S(1)}, bf16[32,2048]{1,0:T(8,128)(2,1)S(1)}, u32[]{:S(2)}, u32[]{:S(2)}) collective-permute-start(bf16[32,2048]{1,0:T(8,128)(2,1)S(1)} %get-tuple-element.433), channel_id=1, source_target_pairs={{0,1},{1,2},{2,3},{3,4},{4,5},{5,6},{6,7},{7,8},{8,9},{9,10},{10,1... | collective-permute-start | bytes 393224 | tf_op jit(solution)/shard_map/while/body/eval_jaxpr/ppermute | solution.py:14
  100.6 6.2 %collective-permute-start = (bf16[32,2048]{1,0:T(8,128)(2,1)S(1)}, bf16[32,2048]{1,0:T(8,128)(2,1)S(1)}, u32[]{:S(2)}, u32[]{:S(2)}) collective-permute-start(bf16[32,2048]{1,0:T(8,128)(2,1)S(1)} %get-tuple-element.433), channel_id=1, source_target_pairs={{0,1},{1,2},{2,3},{3,4},{4,5},{5,6},{6,7},{7,8},{8,9},{9,10},{10,1... | collective-permute-start | bytes 393224 | tf_op jit(solution)/shard_map/while/body/eval_jaxpr/ppermute | solution.py:14
  114.0 6.4 %collective-permute-start = (bf16[32,2048]{1,0:T(8,128)(2,1)S(1)}, bf16[32,2048]{1,0:T(8,128)(2,1)S(1)}, u32[]{:S(2)}, u32[]{:S(2)}) collective-permute-start(bf16[32,2048]{1,0:T(8,128)(2,1)S(1)} %get-tuple-element.433), channel_id=1, source_target_pairs={{0,1},{1,2},{2,3},{3,4},{4,5},{5,6},{6,7},{7,8},{8,9},{9,10},{10,1... | collective-permute-start | bytes 393224 | tf_op jit(solution)/shard_map/while/body/eval_jaxpr/ppermute | solution.py:14
  121.1 12.7 %collective-permute-start = (bf16[32,2048]{1,0:T(8,128)(2,1)S(1)}, bf16[32,2048]{1,0:T(8,128)(2,1)S(1)}, u32[]{:S(2)}, u32[]{:S(2)}) collective-permute-start(bf16[32,2048]{1,0:T(8,128)(2,1)S(1)} %get-tuple-element.433), channel_id=1, source_target_pairs={{0,1},{1,2},{2,3},{3,4},{4,5},{5,6},{6,7},{7,8},{8,9},{9,10},{10,1... | collective-permute-start | bytes 393224 | tf_op jit(solution)/shard_map/while/body/eval_jaxpr/ppermute | solution.py:14
  134.5 6.3 %collective-permute-start = (bf16[32,2048]{1,0:T(8,128)(2,1)S(1)}, bf16[32,2048]{1,0:T(8,128)(2,1)S(1)}, u32[]{:S(2)}, u32[]{:S(2)}) collective-permute-start(bf16[32,2048]{1,0:T(8,128)(2,1)S(1)} %get-tuple-element.433), channel_id=1, source_target_pairs={{0,1},{1,2},{2,3},{3,4},{4,5},{5,6},{6,7},{7,8},{8,9},{9,10},{10,1... | collective-permute-start | bytes 393224 | tf_op jit(solution)/shard_map/while/body/eval_jaxpr/ppermute | solution.py:14
  141.5 12.8 %collective-permute-start = (bf16[32,2048]{1,0:T(8,128)(2,1)S(1)}, bf16[32,2048]{1,0:T(8,128)(2,1)S(1)}, u32[]{:S(2)}, u32[]{:S(2)}) collective-permute-start(bf16[32,2048]{1,0:T(8,128)(2,1)S(1)} %get-tuple-element.433), channel_id=1, source_target_pairs={{0,1},{1,2},{2,3},{3,4},{4,5},{5,6},{6,7},{7,8},{8,9},{9,10},{10,1... | collective-permute-start | bytes 393224 | tf_op jit(solution)/shard_map/while/body/eval_jaxpr/ppermute | solution.py:14
  155.0 6.3 %collective-permute-start = (bf16[32,2048]{1,0:T(8,128)(2,1)S(1)}, bf16[32,2048]{1,0:T(8,128)(2,1)S(1)}, u32[]{:S(2)}, u32[]{:S(2)}) collective-permute-start(bf16[32,2048]{1,0:T(8,128)(2,1)S(1)} %get-tuple-element.433), channel_id=1, source_target_pairs={{0,1},{1,2},{2,3},{3,4},{4,5},{5,6},{6,7},{7,8},{8,9},{9,10},{10,1... | collective-permute-start | bytes 393224 | tf_op jit(solution)/shard_map/while/body/eval_jaxpr/ppermute | solution.py:14
  162.0 8.2 %collective-permute-start = (bf16[32,2048]{1,0:T(8,128)(2,1)S(1)}, bf16[32,2048]{1,0:T(8,128)(2,1)S(1)}, u32[]{:S(2)}, u32[]{:S(2)}) collective-permute-start(bf16[32,2048]{1,0:T(8,128)(2,1)S(1)} %get-tuple-element.433), channel_id=1, source_target_pairs={{0,1},{1,2},{2,3},{3,4},{4,5},{5,6},{6,7},{7,8},{8,9},{9,10},{10,1... | collective-permute-start | bytes 393224 | tf_op jit(solution)/shard_map/while/body/eval_jaxpr/ppermute | solution.py:14
  170.9 7.2 %collective-permute-start = (bf16[32,2048]{1,0:T(8,128)(2,1)S(1)}, bf16[32,2048]{1,0:T(8,128)(2,1)S(1)}, u32[]{:S(2)}, u32[]{:S(2)}) collective-permute-start(bf16[32,2048]{1,0:T(8,128)(2,1)S(1)} %get-tuple-element.433), channel_id=1, source_target_pairs={{0,1},{1,2},{2,3},{3,4},{4,5},{5,6},{6,7},{7,8},{8,9},{9,10},{10,1... | collective-permute-start | bytes 393224 | tf_op jit(solution)/shard_map/while/body/eval_jaxpr/ppermute | solution.py:14
  178.8 13.7 %collective-permute-start = (bf16[32,2048]{1,0:T(8,128)(2,1)S(1)}, bf16[32,2048]{1,0:T(8,128)(2,1)S(1)}, u32[]{:S(2)}, u32[]{:S(2)}) collective-permute-start(bf16[32,2048]{1,0:T(8,128)(2,1)S(1)} %get-tuple-element.433), channel_id=1, source_target_pairs={{0,1},{1,2},{2,3},{3,4},{4,5},{5,6},{6,7},{7,8},{8,9},{9,10},{10,1... | collective-permute-start | bytes 393224 | tf_op jit(solution)/shard_map/while/body/eval_jaxpr/ppermute | solution.py:14
  193.2 7.2 %collective-permute-start = (bf16[32,2048]{1,0:T(8,128)(2,1)S(1)}, bf16[32,2048]{1,0:T(8,128)(2,1)S(1)}, u32[]{:S(2)}, u32[]{:S(2)}) collective-permute-start(bf16[32,2048]{1,0:T(8,128)(2,1)S(1)} %get-tuple-element.433), channel_id=1, source_target_pairs={{0,1},{1,2},{2,3},{3,4},{4,5},{5,6},{6,7},{7,8},{8,9},{9,10},{10,1... | collective-permute-start | bytes 393224 | tf_op jit(solution)/shard_map/while/body/eval_jaxpr/ppermute | solution.py:14
  201.1 7.2 %collective-permute-start = (bf16[32,2048]{1,0:T(8,128)(2,1)S(1)}, bf16[32,2048]{1,0:T(8,128)(2,1)S(1)}, u32[]{:S(2)}, u32[]{:S(2)}) collective-permute-start(bf16[32,2048]{1,0:T(8,128)(2,1)S(1)} %get-tuple-element.433), channel_id=1, source_target_pairs={{0,1},{1,2},{2,3},{3,4},{4,5},{5,6},{6,7},{7,8},{8,9},{9,10},{10,1... | collective-permute-start | bytes 393224 | tf_op jit(solution)/shard_map/while/body/eval_jaxpr/ppermute | solution.py:14
  209.0 7.2 %collective-permute-start = (bf16[32,2048]{1,0:T(8,128)(2,1)S(1)}, bf16[32,2048]{1,0:T(8,128)(2,1)S(1)}, u32[]{:S(2)}, u32[]{:S(2)}) collective-permute-start(bf16[32,2048]{1,0:T(8,128)(2,1)S(1)} %get-tuple-element.433), channel_id=1, source_target_pairs={{0,1},{1,2},{2,3},{3,4},{4,5},{5,6},{6,7},{7,8},{8,9},{9,10},{10,1... | collective-permute-start | bytes 393224 | tf_op jit(solution)/shard_map/while/body/eval_jaxpr/ppermute | solution.py:14
  216.9 7.6 %collective-permute-start = (bf16[32,2048]{1,0:T(8,128)(2,1)S(1)}, bf16[32,2048]{1,0:T(8,128)(2,1)S(1)}, u32[]{:S(2)}, u32[]{:S(2)}) collective-permute-start(bf16[32,2048]{1,0:T(8,128)(2,1)S(1)} %get-tuple-element.433), channel_id=1, source_target_pairs={{0,1},{1,2},{2,3},{3,4},{4,5},{5,6},{6,7},{7,8},{8,9},{9,10},{10,1... | collective-permute-start | bytes 393224 | tf_op jit(solution)/shard_map/while/body/eval_jaxpr/ppermute | solution.py:14
  225.2 7.2 %collective-permute-start = (bf16[32,2048]{1,0:T(8,128)(2,1)S(1)}, bf16[32,2048]{1,0:T(8,128)(2,1)S(1)}, u32[]{:S(2)}, u32[]{:S(2)}) collective-permute-start(bf16[32,2048]{1,0:T(8,128)(2,1)S(1)} %get-tuple-element.433), channel_id=1, source_target_pairs={{0,1},{1,2},{2,3},{3,4},{4,5},{5,6},{6,7},{7,8},{8,9},{9,10},{10,1... | collective-permute-start | bytes 393224 | tf_op jit(solution)/shard_map/while/body/eval_jaxpr/ppermute | solution.py:14
  233.2 7.2 %collective-permute-start = (bf16[32,2048]{1,0:T(8,128)(2,1)S(1)}, bf16[32,2048]{1,0:T(8,128)(2,1)S(1)}, u32[]{:S(2)}, u32[]{:S(2)}) collective-permute-start(bf16[32,2048]{1,0:T(8,128)(2,1)S(1)} %get-tuple-element.433), channel_id=1, source_target_pairs={{0,1},{1,2},{2,3},{3,4},{4,5},{5,6},{6,7},{7,8},{8,9},{9,10},{10,1... | collective-permute-start | bytes 393224 | tf_op jit(solution)/shard_map/while/body/eval_jaxpr/ppermute | solution.py:14
  241.1 7.2 %collective-permute-start = (bf16[32,2048]{1,0:T(8,128)(2,1)S(1)}, bf16[32,2048]{1,0:T(8,128)(2,1)S(1)}, u32[]{:S(2)}, u32[]{:S(2)}) collective-permute-start(bf16[32,2048]{1,0:T(8,128)(2,1)S(1)} %get-tuple-element.433), channel_id=1, source_target_pairs={{0,1},{1,2},{2,3},{3,4},{4,5},{5,6},{6,7},{7,8},{8,9},{9,10},{10,1... | collective-permute-start | bytes 393224 | tf_op jit(solution)/shard_map/while/body/eval_jaxpr/ppermute | solution.py:14
  249.0 8.6 %collective-permute-start = (bf16[32,2048]{1,0:T(8,128)(2,1)S(1)}, bf16[32,2048]{1,0:T(8,128)(2,1)S(1)}, u32[]{:S(2)}, u32[]{:S(2)}) collective-permute-start(bf16[32,2048]{1,0:T(8,128)(2,1)S(1)} %get-tuple-element.433), channel_id=1, source_target_pairs={{0,1},{1,2},{2,3},{3,4},{4,5},{5,6},{6,7},{7,8},{8,9},{9,10},{10,1... | collective-permute-start | bytes 393224 | tf_op jit(solution)/shard_map/while/body/eval_jaxpr/ppermute | solution.py:14
  257.5 64.9 %copy-start = (f32[1,224,2048]{2,1,0:T(8,128)}, f32[1,224,2048]{2,1,0:T(8,128)S(1)}, u32[]{:S(2)}) copy-start(f32[1,224,2048]{2,1,0:T(8,128)S(1)} %get-tuple-element.273) | copy-start | bytes 5505028
